TPU v7x, 128 devices: a whole 4x4x4 slice. The times are simulated.
128 devices in a mesh: dom: 16 (over x, z), grid: 8 (over y, core).
Axes of the slice: x: 4, y: 4, z: 4, core: 2. Of those that a mesh axis runs over, the one named last changes fastest.
Arguments:
- adjoint: float32 [8, 6, 2048, 128], P('grid', None, 'dom'), may hold values from -6 to 6
- jac_diag: float32 [8, 6, 6, 2048, 128], P('grid', None, None, 'dom'), may hold values from -6 to 6
- jac_face: float32 [8, 6, 4, 6, 2048, 128], P('grid', None, None, None, 'dom'), may hold values from -3 to 3
- metric: float32 [8, 6, 3, 4, 2048, 128], P('grid', None, None, None, 'dom'), may hold values from -1.5 to 1.5
- node_id: int32 [8, 4, 2048, 128], P('grid', None, 'dom'), may hold values from 0 to 65535
- fringe_cell: int32 [128, 128, 128], P(('dom', 'grid')), may hold values from 0 to 16383
- donor_cell: int32 [128, 128, 128], P(('dom', 'grid')), may hold values from 0 to 16383
- fringe_weight: float32 [128, 128, 128], P(('dom', 'grid')), may hold values from 0.05 to 1
- donor_count: int32 [128, 128], P(('dom', 'grid')), may hold values from 16 to 128, as said below
Outputs:
- product: float32 [8, 6, 2048, 128], P('grid', None, 'dom')
- node_sens: float32 [3, 65536], P(None, ('dom', 'grid'))
Inputs may be any that keep to these rules, and one draw needn't show every extreme that they name: The live slots from p to q are slots 0 to donor_count[q, p] - 1; in every draw some receiving device has 128 live slots from every sender.
All inputs are finite; a program needn't handle non-finite values.
Results may differ from a plain program's by a relative error of at most 0.000071.
Values sent between devices are 32-bit elements; how exact they have to be, the bound alone decides.
A program may use at most 192 MiB of HBM per device.

v0:
```python
import jax
import jax.numpy as jnp
from jax import lax
from jax.sharding import PartitionSpec as P

NODE_DEV = 512


def shifted(block, axis, distance):
    devices = range(lax.axis_size(axis))
    route = [(i - distance, i) for i in devices if i - distance in devices]
    return lax.ppermute(block, axis, route)


def contract(blocks, adjoint_local):
    running = blocks[0] * adjoint_local[0]
    for variable in range(1, adjoint_local.shape[0]):
        running = running + blocks[variable] * adjoint_local[variable]
    return running


def local(
    adjoint,
    jac_diag,
    jac_face,
    metric,
    node_id,
    fringe_cell,
    donor_cell,
    fringe_weight,
    donor_count,
):
    values = adjoint[0]
    variables, row_count, block_width = values.shape
    diagonal_part = contract(jac_diag[0], values)
    face_terms = contract(jac_face[0], values)
    corner_terms = contract(metric[0], values)
    from_below = shifted(face_terms[0, :, 0, :], "dom", -1)
    from_above = shifted(face_terms[1, :, row_count - 1, :], "dom", 1)
    carried = jnp.concatenate([face_terms[0, :, 1:, :], from_below[:, None, :]], axis=1)
    carried = carried + jnp.concatenate([from_above[:, None, :], face_terms[1, :, :-1, :]], axis=1)
    carried = carried + jnp.pad(face_terms[2, :, :, 1:], ((0, 0), (0, 0), (0, 1)))
    carried = carried + jnp.pad(face_terms[3, :, :, :-1], ((0, 0), (0, 0), (1, 0)))
    flat_values = values.reshape(variables, row_count * block_width)
    payload = jnp.take(flat_values, fringe_cell[0], axis=1)
    capacity = payload.shape[2]
    received = lax.all_to_all(payload, ("dom", "grid"), split_axis=1, concat_axis=1, tiled=True)
    live_slots = jnp.arange(capacity, dtype=jnp.int32)[None, :] < donor_count[0][:, None]
    slot_weights = jnp.where(live_slots, fringe_weight[0], jnp.zeros_like(fringe_weight[0]))
    interp = jnp.zeros((variables, row_count * block_width), jnp.float32)
    interp = interp.at[:, donor_cell[0]].add(-(received * slot_weights[None]))
    product = diagonal_part + carried + interp.reshape(variables, row_count, block_width)
    node_total = NODE_DEV * lax.axis_size("dom") * lax.axis_size("grid")
    partial_value = (
        jnp.zeros((corner_terms.shape[0], node_total), jnp.float32)
        .at[:, node_id[0]]
        .add(corner_terms)
    )
    node_sens = lax.psum_scatter(partial_value, ("dom", "grid"), scatter_dimension=1, tiled=True)
    return (product[None], node_sens)


def solution(mesh):
    in_specs = (
        P("grid", None, "dom", None),
        P("grid", None, None, "dom", None),
        P("grid", None, None, None, "dom", None),
        P("grid", None, None, None, "dom", None),
        P("grid", None, "dom", None),
        P(("dom", "grid"), None, None),
        P(("dom", "grid"), None, None),
        P(("dom", "grid"), None, None),
        P(("dom", "grid"), None),
    )
    out_specs = (P("grid", None, "dom", None), P(None, ("dom", "grid")))
    return jax.shard_map(local, mesh=mesh, in_specs=in_specs, out_specs=out_specs, check_vma=False)
```

profile of v0, /device:TPU:1, one launch (start us, length us, event | category | flops | bytes accessed | tf_op | source)
XLA Modules:
  0.0 1183.3 jit_solution(10600078985395206169)
XLA Ops:
  7.2 1.0 slice_bitcast_fusion.9
  8.2 0.0 copy-start.2
  8.2 0.0 copy-start.4
  8.2 0.0 copy-start.6
  8.2 0.0 copy-start.1
  8.2 4.9 fusion.4
  13.1 1.3 collective-permute-start
  14.4 5.0 collective-permute-start.1
  19.5 4.7 copy.26
  24.2 57.9 %gather_fusion = f32[16384,6]{1,0:T(8,128)} fusion(f32[6,16384]{0,1:T(8,128)} %bitcast.162, s32[16384]{0:T(1024)S(1)} %fusion.27), kind=kCustom, calls=%fused_computation | custom fusion | bytes 851968 | tf_op jit(solution)/shard_map/jit(_take)/gather | solution.py:45
  82.1 5.5 copy.27
  87.6 0.9 select_bitcast_fusion
  88.5 13.2 %all-to-all-start = ((f32[6,128,128]{2,0,1:T(8,128)}), f32[6,128,128]{2,0,1:T(8,128)S(1)}, u32[]{:S(2)}, u32[]{:S(2)}) async-start(f32[6,128,128]{2,0,1:T(8,128)} %select_bitcast_fusion), calls=%async_computation | async-start | bytes 1048576 | tf_op jit(solution)/shard_map/all_to_all | solution.py:47
  101.7 0.0 reduce-scatter.2.cloned.1.call-start
  101.8 2.8 fusion.10
  104.6 16.5 %copy.32 = f32[4,128,128,3]{3,2,1,0:T(8,128)} copy(f32[4,128,128,3]{2,1,0,3:T(8,128)S(1)} %fusion.10) | data formatting | bytes 1572864 | tf_op jit(solution)/shard_map/add | solution.py:18
  121.1 360.6 %scatter_custom_fusion.1 = f32[3,65536]{0,1:T(8,128)} fusion(s32[65536]{0:T(1024)S(1)} %bitcast.164, f32[65536,3]{1,0:T(8,128)} %bitcast.160, f32[]{:T(128)} %constant.7.clone.1), kind=kCustom, calls=%fused_computation.3 | custom fusion | flops 196608 | bytes 786944 | tf_op jit(solution)/shard_map/scatter-add | solution.py:57
  481.7 0.0 reduce-scatter.2.cloned.1.call-update
  481.8 0.8 slice_bitcast_fusion.2
  482.6 1.0 slice_bitcast_fusion.1
  483.6 0.0 copy-done.10
  483.6 0.1 select_bitcast_fusion.1
  483.7 0.0 collective-permute-done
  483.7 0.0 collective-permute-done.1
  483.8 0.0 all-to-all-done
  483.8 0.1 negate_bitcast_fusion
  483.9 5.3 copy.28
  489.1 91.3 %scatter_custom_fusion = f32[6,16384]{0,1:T(8,128)} fusion(s32[16384]{0:T(1024)S(1)} %fusion.25, f32[16384,6]{1,0:T(8,128)} %copy.28, f32[]{:T(128)} %constant.7.clone.1), kind=kCustom, calls=%fused_computation.5 | custom fusion | flops 98304 | bytes 393728 | tf_op jit(solution)/shard_map/scatter-add | solution.py:51
  580.4 5.4 copy.29
  585.9 2.4 fusion.19
  588.4 586.4 %reduce-scatter.2.cloned.1.call-done = f32[3,512]{0,1:T(8,128)} async-done(((f32[3,65536]{0,1:T(8,128)}), f32[3,512]{0,1:T(8,128)}) %reduce-scatter.2.cloned.1.call-update) | async-done | bytes 6160 | tf_op jit(solution)/shard_map/reduce_scatter | solution.py:59
  1174.8 1.7 copy.31
  (26 shorter events, 0.1 us)
Async XLA Ops:
  8.2 93.6 %copy-start.2 = (f32[128,128]{1,0:T(8,128)}, f32[128,128]{1,0:T(8,128)S(1)}, u32[]{:S(2)}) copy-start(f32[128,128]{1,0:T(8,128)S(1)} %get-tuple-element.18) | copy-start | bytes 196612
  8.2 93.6 %copy-start.4 = (f32[128,128]{1,0:T(8,128)}, f32[128,128]{1,0:T(8,128)S(1)}, u32[]{:S(2)}) copy-start(f32[128,128]{1,0:T(8,128)S(1)} %get-tuple-element.19) | copy-start | bytes 196612
  8.2 11.2 copy-start.6
  8.2 11.3 copy-start.1
  13.1 470.6 %collective-permute-start = (f32[6,128]{1,0:T(8,128)S(1)}, f32[6,128]{1,0:T(8,128)S(1)}, u32[]{:S(2)}, u32[]{:S(2)}) collective-permute-start(f32[6,128]{1,0:T(8,128)S(1)} %bitcast.165), channel_id=1, source_target_pairs={{8,0},{16,8},{24,16},{32,24},{40,32},{48,40},{56,48},{64,56},{72,6... | collective-permute-start | bytes 9224 | tf_op jit(solution)/shard_map/ppermute | solution.py:12
  14.4 469.3 %collective-permute-start.1 = (f32[6,128]{1,0:T(8,128)S(1)}, f32[6,128]{1,0:T(8,128)S(1)}, u32[]{:S(2)}, u32[]{:S(2)}) collective-permute-start(f32[6,128]{1,0:T(8,128)S(1)} %bitcast.166), channel_id=1, source_target_pairs={{0,8},{8,16},{16,24},{24,32},{32,40},{40,48},{48,56},{56,64},{64,7... | collective-permute-start | bytes 9224 | tf_op jit(solution)/shard_map/ppermute | solution.py:12
  82.1 19.6 %copy-start.7 = (s32[1,4,128,128]{3,2,1,0:T(8,128)S(1)}, s32[1,4,128,128]{3,2,1,0:T(8,128)}, u32[]{:S(2)}) copy-start(s32[1,4,128,128]{3,2,1,0:T(8,128)} %param.13) | copy-start | bytes 786436
  88.5 395.3 %all-to-all-start = ((f32[6,128,128]{2,0,1:T(8,128)}), f32[6,128,128]{2,0,1:T(8,128)S(1)}, u32[]{:S(2)}, u32[]{:S(2)}) async-start(f32[6,128,128]{2,0,1:T(8,128)} %select_bitcast_fusion), calls=%async_computation | async-start | bytes 1048576 | tf_op jit(solution)/shard_map/all_to_all | solution.py:47
  101.7 1073.2 %reduce-scatter.2.cloned.1.call-start = ((), (), s32[]{:S(2)}) async-start(), calls=%async_computation.2 | async-start | bytes 33816576 | tf_op jit(solution)/shard_map/reduce_scatter | solution.py:59
  481.7 0.9 copy-start.8
  481.7 1.9 copy-start.9
  481.7 1.9 copy-start.10
  580.4 5.5 copy-start
  580.4 5.5 copy-start.3
  580.4 5.5 copy-start.5
Sparse Core Ops, SparseCore 0:
  481.9 692.8 reduce-scatter.1
where the time goes:
time: 1190 us; the launch traced here: 1180 us
  waiting for transfers between devices  586 us (49%)
  other arithmetic  463 us (39%)
  local copies, waits for them, and re-layouts  99.9 us (8%)
  starting transfers between devices  19.5 us (2%)
  between operations  14.3 us (1%)
    reduce_scatter x1, waiting for transfers between devices, local(): lax.psum_scatter(partial_value, ('dom', 'grid'), scatter_dimension=1, til...  586 us
    scatter-add x1, other arithmetic, local(): partial_value = jnp.zeros((corner_terms.shape[0], node_total), jnp.float3...  361 us
    scatter-add x1, other arithmetic, local(): interp = interp.at[:, donor_cell[0]].add(-(received * slot_weights[None]))  91.3 us
    gather x2, local copies, waits for them, and re-layouts, local(): payload = jnp.take(flat_values, fringe_cell[0], axis=1)  63.4 us
  transfers between devices with their start and end apart: 4, of which 1 were waited for; matrix products, arithmetic and copies ran while one was open for 47% of the time, Pallas kernels for 0%

commit v1 on v0

v1 whole, which is shorter than its diff:
```python
import jax
import jax.numpy as jnp
from jax import lax
from jax.experimental import pallas as pl
from jax.experimental.pallas import tpu as pltpu
from jax.sharding import PartitionSpec as P

BF = jnp.bfloat16
F32 = jnp.float32
VMEM_LIMIT = 60 * 2**20


def spread(row, rows):
    tile = jnp.broadcast_to(row, (16, row.shape[1])).astype(BF)
    return jnp.concatenate([tile] * (rows // 16), axis=0)


def ids(rows):
    return lax.broadcasted_iota(jnp.int32, (rows, 128), 0).astype(F32).astype(BF)


def halves(value):
    high = value.astype(BF).astype(F32)
    return high, value - high


def onehot(mask):
    return jnp.where(mask, jnp.ones((), BF), jnp.zeros((), BF))


def gather_kernel(adj_ref, cell_ref, out_ref, table):
    step = pl.program_id(0)

    @pl.when(step == 0)
    def _():
        for v in range(6):
            high, low = halves(adj_ref[v])
            table[v * 128:(v + 1) * 128, :128] = high.astype(BF)
            table[v * 128:(v + 1) * 128, 128:] = low.astype(BF)

    lane_ids = ids(128)
    row_ids = lax.broadcasted_iota(jnp.int32, (128, 128), 0)
    cells = cell_ref[...]
    rows, lanes = cells >> 7, (cells & 127).astype(F32)
    for pair in range(4):
        js = (2 * pair, 2 * pair + 1)
        pick = jnp.concatenate([onehot(lane_ids == spread(lanes[j:j + 1], 128)) for j in js], 1)
        pick = jnp.concatenate([pick, pick], 0)
        hits = [row_ids == jnp.broadcast_to(rows[j:j + 1], (128, 128)) for j in js]
        for v in range(6):
            found = jnp.dot(table[v * 128:(v + 1) * 128, :], pick, preferred_element_type=F32)
            for side, j in enumerate(js):
                part = jnp.where(hits[side], found[:, side * 128:(side + 1) * 128], 0.0)
                out_ref[j, v:v + 1, :] = jnp.sum(part, axis=0, keepdims=True)


def gather(adj, cells):
    return pl.pallas_call(
        gather_kernel,
        grid=(16,),
        in_specs=[
            pl.BlockSpec((6, 128, 128), lambda s: (0, 0, 0)),
            pl.BlockSpec((8, 128), lambda s: (s, 0)),
        ],
        out_specs=pl.BlockSpec((8, 6, 128), lambda s: (s, 0, 0)),
        out_shape=jax.ShapeDtypeStruct((128, 6, 128), F32),
        scratch_shapes=[pltpu.VMEM((768, 256), BF)],
        compiler_params=pltpu.CompilerParams(vmem_limit_bytes=VMEM_LIMIT),
        cost_estimate=pl.CostEstimate(flops=6 * 10**9, bytes_accessed=10**6, transcendentals=0),
        name="fringe_gather",
    )(adj, cells)


def node_kernel(adj_ref, met_ref, nid_ref, out_ref, acc):
    step = pl.program_id(0)

    @pl.when(step == 0)
    def _():
        acc[...] = jnp.zeros_like(acc)

    row_ids = ids(256)
    zero = jnp.zeros((256, 128), BF)
    depth = 4

    def corner(k, carry):
        n = nid_ref[k]
        high = (((n >> 8) & 1) * 128 + (n >> 9)).astype(F32)
        low = (n & 255).astype(F32)
        terms = []
        for x in range(3):
            term = met_ref[0, x, k] * adj_ref[0]
            for i in range(1, 6):
                term = term + met_ref[i, x, k] * adj_ref[i]
            terms += halves(term)
        for group in range(8 // depth):
            js = range(group * depth, (group + 1) * depth)
            lows = jnp.concatenate([onehot(row_ids == spread(low[j:j + 1], 256)) for j in js], 1)
            masks = [row_ids == spread(high[j:j + 1], 256) for j in js]
            for t in range(6):
                highs = jnp.concatenate(
                    [jnp.where(m, spread(terms[t][j:j + 1], 256), zero) for m, j in zip(masks, js)], 1
                )
                acc[t] += lax.dot_general(
                    highs, lows, (((1,), (1,)), ((), ())), preferred_element_type=F32
                )
        return carry

    lax.fori_loop(0, 4, corner, 0)

    @pl.when(step == pl.num_programs(0) - 1)
    def _():
        out_ref[...] = jnp.zeros_like(out_ref)
        for x in range(3):
            for e in range(2):
                both = acc[2 * x, e * 128:(e + 1) * 128, :] + acc[2 * x + 1, e * 128:(e + 1) * 128, :]
                for b in range(2):
                    out_ref[pl.ds(x * 4 + e * 2 + b, 128, stride=16), :] = both[:, b * 128:(b + 1) * 128]


def node_partial(adj, metric, node_id):
    return pl.pallas_call(
        node_kernel,
        grid=(16,),
        in_specs=[
            pl.BlockSpec((6, 8, 128), lambda s: (0, s, 0)),
            pl.BlockSpec((6, 3, 4, 8, 128), lambda s: (0, 0, 0, s, 0)),
            pl.BlockSpec((4, 8, 128), lambda s: (0, s, 0)),
        ],
        out_specs=pl.BlockSpec((2048, 128), lambda s: (0, 0)),
        out_shape=jax.ShapeDtypeStruct((2048, 128), F32),
        scratch_shapes=[pltpu.VMEM((6, 256, 256), F32)],
        compiler_params=pltpu.CompilerParams(vmem_limit_bytes=VMEM_LIMIT),
        cost_estimate=pl.CostEstimate(flops=52 * 10**9, bytes_accessed=6 * 10**6, transcendentals=0),
        name="node_scatter",
    )(adj, metric, node_id)


def interp_kernel(recv_ref, cell_ref, weight_ref, count_ref, out_ref, acc):
    step = pl.program_id(0)

    @pl.when(step == 0)
    def _():
        acc[...] = jnp.zeros_like(acc)

    ids_low, ids_high = ids(256), ids(64)
    zero = jnp.zeros((64, 128), BF)
    depth = 4

    def senders(block, carry):
        rows8 = pl.ds(block * 8, 8)
        cells = cell_ref[rows8]
        rows, cols = cells >> 7, cells & 127
        high = (rows & 63).astype(F32)
        low = ((rows >> 6) * 128 + cols).astype(F32)
        live = lax.broadcasted_iota(jnp.int32, (8, 128), 1) < count_ref[rows8]
        weights = jnp.where(live, weight_ref[rows8], 0.0)
        values = [halves(-(recv_ref[rows8, i, :] * weights)) for i in range(6)]
        for group in range(8 // depth):
            js = range(group * depth, (group + 1) * depth)
            lows = jnp.concatenate([onehot(ids_low == spread(low[j:j + 1], 256)) for j in js], 1)
            masks = [ids_high == spread(high[j:j + 1], 64) for j in js]
            for third in range(3):
                highs = jnp.concatenate(
                    [
                        jnp.concatenate(
                            [jnp.where(m, spread(values[i][part][j:j + 1], 64), zero) for m, j in zip(masks, js)], 1
                        )
                        for i in (2 * third, 2 * third + 1)
                        for part in range(2)
                    ],
                    0,
                )
                acc[third] += lax.dot_general(
                    highs, lows, (((1,), (1,)), ((), ())), preferred_element_type=F32
                )
        return carry

    lax.fori_loop(0, 4, senders, 0)

    @pl.when(step == pl.num_programs(0) - 1)
    def _():
        for i in range(6):
            start = (i % 2) * 128
            both = acc[i // 2, start:start + 64, :] + acc[i // 2, start + 64:start + 128, :]
            out_ref[i, :64, :] = both[:, :128]
            out_ref[i, 64:, :] = both[:, 128:]


def interpolate(received, cells, weights, counts):
    return pl.pallas_call(
        interp_kernel,
        grid=(4,),
        in_specs=[
            pl.BlockSpec((32, 6, 128), lambda s: (s, 0, 0)),
            pl.BlockSpec((32, 128), lambda s: (s, 0)),
            pl.BlockSpec((32, 128), lambda s: (s, 0)),
            pl.BlockSpec((32, 1), lambda s: (s, 0)),
        ],
        out_specs=pl.BlockSpec((6, 128, 128), lambda s: (0, 0, 0)),
        out_shape=jax.ShapeDtypeStruct((6, 128, 128), F32),
        scratch_shapes=[pltpu.VMEM((3, 256, 256), F32)],
        compiler_params=pltpu.CompilerParams(vmem_limit_bytes=VMEM_LIMIT),
        cost_estimate=pl.CostEstimate(flops=6 * 10**9, bytes_accessed=10**6, transcendentals=0),
        name="donor_scatter",
    )(received, cells, weights, counts)


def shifted(block, axis, distance):
    devices = range(lax.axis_size(axis))
    route = [(i - distance, i) for i in devices if i - distance in devices]
    return lax.ppermute(block, axis, route)


def contract(blocks, adjoint_local):
    running = blocks[0] * adjoint_local[0]
    for variable in range(1, adjoint_local.shape[0]):
        running = running + blocks[variable] * adjoint_local[variable]
    return running


def local(
    adjoint,
    jac_diag,
    jac_face,
    metric,
    node_id,
    fringe_cell,
    donor_cell,
    fringe_weight,
    donor_count,
):
    values = adjoint[0]
    row_count = values.shape[1]
    payload = gather(values, fringe_cell[0])
    received = lax.all_to_all(payload, ("dom", "grid"), split_axis=0, concat_axis=0, tiled=True)
    partial_value = node_partial(values, metric[0], node_id[0])
    owned = lax.psum_scatter(partial_value, ("dom", "grid"), scatter_dimension=0, tiled=True)
    node_sens = owned[:12].reshape(3, 512)

    diagonal_part = contract(jac_diag[0], values)
    face_terms = contract(jac_face[0], values)
    from_below = shifted(face_terms[0, :, 0, :], "dom", -1)
    from_above = shifted(face_terms[1, :, row_count - 1, :], "dom", 1)
    carried = jnp.concatenate([face_terms[0, :, 1:, :], from_below[:, None, :]], axis=1)
    carried = carried + jnp.concatenate([from_above[:, None, :], face_terms[1, :, :-1, :]], axis=1)
    carried = carried + jnp.pad(face_terms[2, :, :, 1:], ((0, 0), (0, 0), (0, 1)))
    carried = carried + jnp.pad(face_terms[3, :, :, :-1], ((0, 0), (0, 0), (1, 0)))
    interp = interpolate(received, donor_cell[0], fringe_weight[0], donor_count.reshape(128, 1))
    product = diagonal_part + carried + interp
    return (product[None], node_sens)


def solution(mesh):
    in_specs = (
        P("grid", None, "dom", None),
        P("grid", None, None, "dom", None),
        P("grid", None, None, None, "dom", None),
        P("grid", None, None, None, "dom", None),
        P("grid", None, "dom", None),
        P(("dom", "grid"), None, None),
        P(("dom", "grid"), None, None),
        P(("dom", "grid"), None, None),
        P(("dom", "grid"), None),
    )
    out_specs = (P("grid", None, "dom", None), P(None, ("dom", "grid")))
    return jax.shard_map(local, mesh=mesh, in_specs=in_specs, out_specs=out_specs, check_vma=False)
```

time: 1190 us -> 734 us (0.62)
  other arithmetic: 463 us -> 7.1 us
  local copies, waits for them, and re-layouts: 99.9 us -> 3.91 us
  Pallas kernels: 0 us -> 92.7 us
    scatter-add x2 -> x0, other arithmetic: 452 us -> none  [the longest x1 361 us: local(): partial_value = jnp.zeros((corner_terms.shape[0], node_total), jnp.float3...]
    pallas_call x0 -> x3, Pallas kernels: none -> 92.7 us  [the longest x1 68.5 us: node_partial(): pl.pallas_call(node_kernel, grid=(16,), in_specs=[pl.BlockSpec((6, 8, 128...]
    gather x2 -> x0, local copies, waits for them, and re-layouts: 63.4 us -> none  [local(): payload = jnp.take(flat_values, fringe_cell[0], axis=1)]
    add x1 -> x0, local copies, waits for them, and re-layouts: 16.5 us -> none  [contract(): running = running + blocks[variable] * adjoint_local[variable]]
  transfers between devices with their start and end apart: 4 -> 4, of which waited for: 1 -> 2; matrix products, arithmetic and copies ran while one was open for 47% -> 1% of each run, Pallas kernels for 0% -> 3%
where the time goes in v1:
time: 734 us; the launch traced here: 727 us
  waiting for transfers between devices  591 us (81%)
  Pallas kernels  92.7 us (13%)
  starting transfers between devices  17.8 us (2%)
  between operations  14.2 us (2%)
    reduce_scatter x1, waiting for transfers between devices, local(): lax.psum_scatter(partial_value, ('dom', 'grid'), scatter_dimension=0, til...  581 us
    pallas_call x1, Pallas kernels, node_partial(): pl.pallas_call(node_kernel, grid=(16,), in_specs=[pl.BlockSpec((6, 8, 128...  68.5 us
  transfers between devices with their start and end apart: 4, of which 2 were waited for; matrix products, arithmetic and copies ran while one was open for 1% of the time, Pallas kernels for 3%

profile of v1, /device:TPU:1, one launch (start us, length us, event | category | flops | bytes accessed | tf_op | source)
XLA Modules:
  0.0 727.0 jit_solution(15515319572526833619)
XLA Ops:
  7.2 0.0 reduce-scatter.2.cloned.1.call-start
  7.2 0.0 copy-start.4
  7.2 68.5 %node_scatter.1 = f32[2048,128]{1,0:T(8,128)} custom-call(f32[6,128,128]{2,1,0:T(8,128)} %bitcast.102, f32[6,3,4,128,128]{4,3,2,1,0:T(8,128)} %bitcast.108, s32[4,128,128]{2,1,0:T(8,128)} %bitcast.109), custom_call_target="tpu_custom_call" | custom-call | flops 51999997952 | bytes 6000000 | tf_op jit(solution)/shard_map/node_scatter/pallas_call | solution.py:121
  75.7 0.0 reduce-scatter.2.cloned.1.call-update
  75.8 0.0 copy-done.4
  75.8 0.0 copy-start.1
  75.8 0.0 copy-start.2
  75.8 0.0 copy-start.3
  75.8 4.9 fusion
  80.7 0.0 copy-done.1
  80.7 0.0 copy-done.2
  80.7 0.0 copy-done.3
  80.8 4.3 collective-permute-start.1
  85.1 1.3 collective-permute-start
  86.4 12.1 %fringe_gather.1 = f32[128,6,128]{2,1,0:T(8,128)} custom-call(f32[6,128,128]{2,1,0:T(8,128)} %bitcast.103, s32[128,128]{1,0:T(8,128)} %bitcast.110), custom_call_target="tpu_custom_call" | custom-call | flops 6000000000 | bytes 1000000 | tf_op jit(solution)/shard_map/fringe_gather/pallas_call | solution.py:58
  98.5 12.1 %all-to-all-start = ((f32[128,6,128]{2,1,0:T(8,128)}), f32[128,6,128]{2,1,0:T(8,128)}, u32[]{:S(2)}, u32[]{:S(2)}) async-start(f32[128,6,128]{2,1,0:T(8,128)} %fringe_gather.1), calls=%async_computation | async-start | bytes 1048576 | tf_op jit(solution)/shard_map/all_to_all | solution.py:235
  110.6 0.0 copy-start.5
  110.6 0.2 slice_bitcast_fusion.1
  110.8 0.1 slice_bitcast_fusion.2
  110.9 0.4 copy-done.5
  111.3 0.7 copy.13.count_ref
  112.0 0.0 collective-permute-done.1
  112.0 0.6 broadcast_in_dim.10
  112.6 0.0 collective-permute-done
  112.6 0.6 broadcast_in_dim.9
  113.2 10.5 %all-to-all-done.recv_ref = f32[128,6,128]{2,1,0:T(8,128)} async-done(((f32[128,6,128]{2,1,0:T(8,128)}), f32[128,6,128]{2,1,0:T(8,128)}, u32[]{:S(2)}, u32[]{:S(2)}) %all-to-all-start) | async-done | bytes 393248 | tf_op jit(solution)/shard_map/all_to_all | solution.py:235
  123.7 0.0 copy-start
  123.7 12.1 %donor_scatter.1 = f32[6,128,128]{2,1,0:T(8,128)} custom-call(f32[128,6,128]{2,1,0:T(8,128)} %all-to-all-done.recv_ref, s32[128,128]{1,0:T(8,128)} %bitcast.111, f32[128,128]{1,0:T(8,128)} %bitcast.112, s32[128,1]{1,0:T(8,128)} %copy.13.count_ref), custom_call_target="tpu_custom_call" | custom-call | flops 6000000000 | bytes 1000000 | tf_op jit(solution)/shard_map/donor_scatter/pallas_call | solution.py:190
  135.8 0.0 copy-done
  135.8 2.2 fusion.9
  138.0 580.8 %reduce-scatter.2.cloned.1.call-done = f32[16,128]{1,0:T(8,128)} async-done(((f32[2048,128]{1,0:T(8,128)}), f32[16,128]{1,0:T(8,128)}) %reduce-scatter.2.cloned.1.call-update) | async-done | bytes 8208 | tf_op jit(solution)/shard_map/reduce_scatter | solution.py:237
  718.8 1.3 reshape.53
  (4 shorter events, 0.0 us)
Async XLA Ops:
  7.2 711.6 %reduce-scatter.2.cloned.1.call-start = ((), (), s32[]{:S(2)}) async-start(), calls=%async_computation.2 | async-start | bytes 1056768 | tf_op jit(solution)/shard_map/reduce_scatter | solution.py:237
  7.2 68.6 %copy-start.4 = (f32[1,6,128,128]{3,2,1,0:T(8,128)S(1)}, f32[1,6,128,128]{3,2,1,0:T(8,128)}, u32[]{:S(2)}) copy-start(f32[1,6,128,128]{3,2,1,0:T(8,128)} %param.9) | copy-start | bytes 1179652
  75.8 4.9 copy-start.1
  75.8 4.9 copy-start.2
  75.8 4.9 copy-start.3
  80.8 31.3 %collective-permute-start.1 = (f32[6,128]{1,0:T(8,128)S(1)}, f32[6,128]{1,0:T(8,128)S(1)}, u32[]{:S(2)}, u32[]{:S(2)}) collective-permute-start(f32[6,128]{1,0:T(8,128)S(1)} %bitcast.105), channel_id=1, source_target_pairs={{0,8},{8,16},{16,24},{24,32},{32,40},{40,48},{48,56},{56,64},{64,7... | collective-permute-start | bytes 9224 | tf_op jit(solution)/shard_map/ppermute | solution.py:211
  85.1 27.5 %collective-permute-start = (f32[6,128]{1,0:T(8,128)S(1)}, f32[6,128]{1,0:T(8,128)S(1)}, u32[]{:S(2)}, u32[]{:S(2)}) collective-permute-start(f32[6,128]{1,0:T(8,128)S(1)} %bitcast.106), channel_id=1, source_target_pairs={{8,0},{16,8},{24,16},{32,24},{40,32},{48,40},{56,48},{64,56},{72,6... | collective-permute-start | bytes 9224 | tf_op jit(solution)/shard_map/ppermute | solution.py:211
  98.5 25.2 %all-to-all-start = ((f32[128,6,128]{2,1,0:T(8,128)}), f32[128,6,128]{2,1,0:T(8,128)}, u32[]{:S(2)}, u32[]{:S(2)}) async-start(f32[128,6,128]{2,1,0:T(8,128)} %fringe_gather.1), calls=%async_computation | async-start | bytes 1048576 | tf_op jit(solution)/shard_map/all_to_all | solution.py:235
  110.6 0.7 copy-start.5
  123.7 12.1 %copy-start = (f32[1,6,6,128,128]{4,3,2,1,0:T(8,128)S(1)}, f32[1,6,6,128,128]{4,3,2,1,0:T(8,128)}, u32[]{:S(2)}) copy-start(f32[1,6,6,128,128]{4,3,2,1,0:T(8,128)} %param.10) | copy-start | bytes 7077892
Sparse Core Ops, SparseCore 0:
  75.9 642.8 reduce-scatter.1

commit v2 on v1

--- a/solution.py
+++ b/solution.py
@@ -234,8 +234,8 @@
     payload = gather(values, fringe_cell[0])
     received = lax.all_to_all(payload, ("dom", "grid"), split_axis=0, concat_axis=0, tiled=True)
     partial_value = node_partial(values, metric[0], node_id[0])
-    owned = lax.psum_scatter(partial_value, ("dom", "grid"), scatter_dimension=0, tiled=True)
-    node_sens = owned[:12].reshape(3, 512)
+    parts = lax.all_to_all(partial_value, ("dom", "grid"), split_axis=0, concat_axis=0, tiled=True)
+    node_sens = jnp.sum(parts.reshape(128, 16, 128), axis=0)[:12].reshape(3, 512)
 
     diagonal_part = contract(jac_diag[0], values)
     face_terms = contract(jac_face[0], values)

time: 734 us -> 136 us (0.19)
  waiting for transfers between devices: 591 us -> 1.68 us
  between operations: 14.2 us -> 0.87 us
  starting transfers between devices: 17.8 us -> 27 us
    reduce_scatter x1 -> x0, waiting for transfers between devices: 581 us -> none  [local(): lax.psum_scatter(partial_value, ('dom', 'grid'), scatter_dimension=0, til...]
    all_to_all x1, waiting for transfers between devices: 10.5 us -> 0.01 us  [local(): lax.all_to_all(payload, ('dom', 'grid'), split_axis=0, concat_axis=0, til...]
    all_to_all x0 -> x1, starting transfers between devices: none -> 9.75 us  [local(): lax.all_to_all(partial_value, ('dom', 'grid'), split_axis=0, concat_axis=...]
  transfers between devices with their start and end apart: 4 -> 4, of which waited for: 2 -> 1; matrix products, arithmetic and copies ran while one was open for 1% -> 4% of each run, Pallas kernels for 3% -> 68%
where the time goes in v2:
time: 136 us; the launch traced here: 135 us
  Pallas kernels  92.5 us (68%)
  starting transfers between devices  27 us (20%)
  other arithmetic  7.93 us (6%)
  local copies, waits for them, and re-layouts  5.02 us (4%)
  waiting for transfers between devices  1.68 us (1%)
    pallas_call x1, Pallas kernels, node_partial(): pl.pallas_call(node_kernel, grid=(16,), in_specs=[pl.BlockSpec((6, 8, 128...  68.5 us
    pallas_call x1, Pallas kernels, gather(): pl.pallas_call(gather_kernel, grid=(16,), in_specs=[pl.BlockSpec((6, 128,...  12.1 us
    pallas_call x1, Pallas kernels, interpolate(): pl.pallas_call(interp_kernel, grid=(4,), in_specs=[pl.BlockSpec((32, 6, 1...  12 us
    all_to_all x1, starting transfers between devices, local(): lax.all_to_all(payload, ('dom', 'grid'), split_axis=0, concat_axis=0, til...  11.6 us
    all_to_all x1, starting transfers between devices, local(): lax.all_to_all(partial_value, ('dom', 'grid'), split_axis=0, concat_axis=...  9.75 us
    ppermute x2, starting transfers between devices, shifted(): return lax.ppermute(block, axis, route)  5.65 us
    add x1, other arithmetic, contract(): running = running + blocks[variable] * adjoint_local[variable]  4.86 us
    broadcast_in_dim x1, other arithmetic, local(): return (product[None], node_sens)  2.92 us
  transfers between devices with their start and end apart: 4, of which 1 were waited for; matrix products, arithmetic and copies ran while one was open for 4% of the time, Pallas kernels for 68%

profile of v2, /device:TPU:1, one launch (start us, length us, event | category | flops | bytes accessed | tf_op | source)
XLA Modules:
  0.0 135.1 jit_solution(126356826061633732)
XLA Ops:
  0.6 1.0 slice_bitcast_fusion.9
  1.7 0.0 copy-start.2
  1.7 0.0 copy-start.4
  1.7 0.0 copy-start.6
  1.7 0.0 copy-start.8
  1.7 4.9 %fusion = f32[4,6,128,128]{3,2,1,0:T(8,128)S(1)} fusion(f32[1,6,4,6,128,128]{5,4,3,2,1,0:T(8,128)} %param.11, f32[128,128]{1,0:T(8,128)S(1)} %get-tuple-element.13, f32[128,128]{1,0:T(8,128)S(1)} %get-tuple-element.9, f32[128,128]{1,0:T(8,128)S(1)} %get-tuple-element.10, f32[128,128]{1,0:T(8,128)S(1)} %get-tuple-element.11, ...), kind=kLoop, calls=%fused_computation.1 | loop fusion | flops 4325376 | bytes 11403264 | tf_op jit(solution)/shard_map/add | solution.py:217
  6.6 0.0 copy-done.2
  6.6 0.0 copy-done.4
  6.6 0.0 copy-done.6
  6.6 4.4 %collective-permute-start.1 = (f32[6,128]{1,0:T(8,128)S(1)}, f32[6,128]{1,0:T(8,128)S(1)}, u32[]{:S(2)}, u32[]{:S(2)}) collective-permute-start(f32[6,128]{1,0:T(8,128)S(1)} %bitcast.107), channel_id=1, source_target_pairs={{0,8},{8,16},{16,24},{24,32},{32,40},{40,48},{48,56},{56,64},{64,7... | collective-permute-start | bytes 9224 | tf_op jit(solution)/shard_map/ppermute | solution.py:211
  11.0 1.3 collective-permute-start
  12.3 12.1 %fringe_gather.1 = f32[128,6,128]{2,1,0:T(8,128)} custom-call(f32[6,128,128]{2,1,0:T(8,128)} %bitcast.104, s32[128,128]{1,0:T(8,128)} %bitcast.112), custom_call_target="tpu_custom_call" | custom-call | flops 6000000000 | bytes 1000000 | tf_op jit(solution)/shard_map/fringe_gather/pallas_call | solution.py:58
  24.4 11.6 %all-to-all-start = ((f32[128,6,128]{2,1,0:T(8,128)}), f32[128,6,128]{2,1,0:T(8,128)S(1)}, u32[]{:S(2)}, u32[]{:S(2)}) async-start(f32[128,6,128]{2,1,0:T(8,128)} %fringe_gather.1), calls=%async_computation | async-start | bytes 1048576 | tf_op jit(solution)/shard_map/all_to_all | solution.py:235
  36.1 68.5 %node_scatter.1 = f32[2048,128]{1,0:T(8,128)} custom-call(f32[6,128,128]{2,1,0:T(8,128)} %bitcast.105, f32[6,3,4,128,128]{4,3,2,1,0:T(8,128)} %bitcast.110, s32[4,128,128]{2,1,0:T(8,128)} %bitcast.111), custom_call_target="tpu_custom_call" | custom-call | flops 51999997952 | bytes 6000000 | tf_op jit(solution)/shard_map/node_scatter/pallas_call | solution.py:121
  104.5 0.2 slice_bitcast_fusion.1
  104.7 0.0 all-to-all-done.recv_ref
  104.7 0.0 copy-start.10
  104.7 0.8 copy-done.10
  105.6 9.7 %all-to-all-start.1 = ((f32[128,16,128]{2,1,0:T(8,128)}), f32[128,16,128]{2,1,0:T(8,128)S(1)}, u32[]{:S(2)}, u32[]{:S(2)}) async-start(f32[128,16,128]{2,1,0:T(8,128)} %bitcast.103), calls=%async_computation.1 | async-start | bytes 2097152 | tf_op jit(solution)/shard_map/all_to_all | solution.py:237
  115.3 1.0 slice_bitcast_fusion.2
  116.3 1.4 %copy.13.count_ref = s32[128,1]{1,0:T(8,128)} copy(s32[128,1]{0,1:T(1,128)} %bitcast.109) | data formatting | bytes 1024 | tf_op jit(solution)/shard_map/reshape | solution.py:248
  117.6 0.0 collective-permute-done.1
  117.6 0.0 collective-permute-done
  117.7 12.0 %donor_scatter.1 = f32[6,128,128]{2,1,0:T(8,128)} custom-call(f32[128,6,128]{2,1,0:T(8,128)} %copy-done.10, s32[128,128]{1,0:T(8,128)} %bitcast.113, f32[128,128]{1,0:T(8,128)} %bitcast.114, s32[128,1]{1,0:T(8,128)} %copy.13.count_ref), custom_call_target="tpu_custom_call" | custom-call | flops 6000000000 | bytes 1000000 | tf_op jit(solution)/shard_map/donor_scatter/pallas_call | solution.py:190
  129.7 0.0 copy-done.3
  129.7 0.0 copy-done.5
  129.7 0.0 copy-done.7
  129.7 0.0 copy-done.9
  129.7 2.9 %fusion.9 = f32[1,6,128,128]{3,2,1,0:T(8,128)} fusion(f32[6,128,128]{2,1,0:T(8,128)} %donor_scatter.1, f32[6,1,128]{2,1,0:T(1,128)S(1)} %broadcast_in_dim.9, f32[6,127,128]{2,1,0:T(8,128)S(1)} %copy-done.1, f32[6,127,128]{2,1,0:T(8,128)S(1)} %copy-done, f32[6,1,128]{2,1,0:T(1,128)S(1)} %broadcast_in_dim.10, f32[6,128,127]{2,1,0:T(8,128)S(1)} %get-tuple-element.3, ...), kind=kLoop, calls=%fused_computation.20 | loop fusion | flops 1769472 | bytes 5105664 | tf_op jit(solution)/shard_map/broadcast_in_dim | solution.py:250
  132.7 1.7 %all-to-all-done.1 = f32[128,16,128]{2,1,0:T(8,128)S(1)} async-done(((f32[128,16,128]{2,1,0:T(8,128)}), f32[128,16,128]{2,1,0:T(8,128)S(1)}, u32[]{:S(2)}, u32[]{:S(2)}) %all-to-all-start.1) | async-done | bytes 1048608 | tf_op jit(solution)/shard_map/all_to_all | solution.py:237
  134.3 0.1 reduce_sum.9
  134.5 0.6 reshape.57
  (14 shorter events, 0.0 us)
Async XLA Ops:
  1.7 4.9 %copy-start.2 = (f32[128,128]{1,0:T(8,128)}, f32[128,128]{1,0:T(8,128)S(1)}, u32[]{:S(2)}) copy-start(f32[128,128]{1,0:T(8,128)S(1)} %get-tuple-element.10) | copy-start | bytes 196612
  1.7 4.9 %copy-start.4 = (f32[128,128]{1,0:T(8,128)}, f32[128,128]{1,0:T(8,128)S(1)}, u32[]{:S(2)}) copy-start(f32[128,128]{1,0:T(8,128)S(1)} %get-tuple-element.11) | copy-start | bytes 196612
  1.7 4.9 %copy-start.6 = (f32[128,128]{1,0:T(8,128)}, f32[128,128]{1,0:T(8,128)S(1)}, u32[]{:S(2)}) copy-start(f32[128,128]{1,0:T(8,128)S(1)} %get-tuple-element.12) | copy-start | bytes 196612
  1.7 4.9 %copy-start.8 = (f32[128,128]{1,0:T(8,128)}, f32[128,128]{1,0:T(8,128)S(1)}, u32[]{:S(2)}) copy-start(f32[128,128]{1,0:T(8,128)S(1)} %get-tuple-element.13) | copy-start | bytes 196612
  6.6 111.0 %collective-permute-start.1 = (f32[6,128]{1,0:T(8,128)S(1)}, f32[6,128]{1,0:T(8,128)S(1)}, u32[]{:S(2)}, u32[]{:S(2)}) collective-permute-start(f32[6,128]{1,0:T(8,128)S(1)} %bitcast.107), channel_id=1, source_target_pairs={{0,8},{8,16},{16,24},{24,32},{32,40},{40,48},{48,56},{56,64},{64,7... | collective-permute-start | bytes 9224 | tf_op jit(solution)/shard_map/ppermute | solution.py:211
  11.0 106.6 %collective-permute-start = (f32[6,128]{1,0:T(8,128)S(1)}, f32[6,128]{1,0:T(8,128)S(1)}, u32[]{:S(2)}, u32[]{:S(2)}) collective-permute-start(f32[6,128]{1,0:T(8,128)S(1)} %bitcast.108), channel_id=1, source_target_pairs={{8,0},{16,8},{24,16},{32,24},{40,32},{48,40},{56,48},{64,56},{72,6... | collective-permute-start | bytes 9224 | tf_op jit(solution)/shard_map/ppermute | solution.py:211
  24.4 80.3 %all-to-all-start = ((f32[128,6,128]{2,1,0:T(8,128)}), f32[128,6,128]{2,1,0:T(8,128)S(1)}, u32[]{:S(2)}, u32[]{:S(2)}) async-start(f32[128,6,128]{2,1,0:T(8,128)} %fringe_gather.1), calls=%async_computation | async-start | bytes 1048576 | tf_op jit(solution)/shard_map/all_to_all | solution.py:235
  104.7 0.8 copy-start.10
  105.6 28.8 %all-to-all-start.1 = ((f32[128,16,128]{2,1,0:T(8,128)}), f32[128,16,128]{2,1,0:T(8,128)S(1)}, u32[]{:S(2)}, u32[]{:S(2)}) async-start(f32[128,16,128]{2,1,0:T(8,128)} %bitcast.103), calls=%async_computation.1 | async-start | bytes 2097152 | tf_op jit(solution)/shard_map/all_to_all | solution.py:237
  117.7 12.0 %copy-start = (f32[6,127,128]{2,1,0:T(8,128)S(1)}, f32[6,127,128]{2,1,0:T(8,128)}, u32[]{:S(2)}) copy-start(f32[6,127,128]{2,1,0:T(8,128)} %get-tuple-element.6) | copy-start | bytes 1170436
  117.7 12.0 %copy-start.1 = (f32[6,127,128]{2,1,0:T(8,128)S(1)}, f32[6,127,128]{2,1,0:T(8,128)}, u32[]{:S(2)}) copy-start(f32[6,127,128]{2,1,0:T(8,128)} %get-tuple-element.7) | copy-start | bytes 1170436
  117.7 12.0 %copy-start.3 = (f32[128,128]{1,0:T(8,128)S(1)}, f32[128,128]{1,0:T(8,128)}, u32[]{:S(2)}) copy-start(f32[128,128]{1,0:T(8,128)} %copy-done.2) | copy-start | bytes 196612
  117.7 12.0 %copy-start.5 = (f32[128,128]{1,0:T(8,128)S(1)}, f32[128,128]{1,0:T(8,128)}, u32[]{:S(2)}) copy-start(f32[128,128]{1,0:T(8,128)} %copy-done.4) | copy-start | bytes 196612
  117.7 12.0 %copy-start.7 = (f32[128,128]{1,0:T(8,128)S(1)}, f32[128,128]{1,0:T(8,128)}, u32[]{:S(2)}) copy-start(f32[128,128]{1,0:T(8,128)} %copy-done.6) | copy-start | bytes 196612
  117.7 12.0 %copy-start.9 = (f32[128,128]{1,0:T(8,128)S(1)}, f32[128,128]{1,0:T(8,128)}, u32[]{:S(2)}) copy-start(f32[128,128]{1,0:T(8,128)} %copy-done.8) | copy-start | bytes 196612

commit v3 on v0

v3 whole, which is shorter than its diff:
```python
import jax
import jax.numpy as jnp
from jax import lax
from jax.experimental import pallas as pl
from jax.experimental.pallas import tpu as pltpu
from jax.sharding import PartitionSpec as P

BF = jnp.bfloat16
F32 = jnp.float32
DEVICES = 128
GRIDS = 8
DOMS = 16
MESH = pl.DeviceIdType.MESH


def spread(row, rows):
    tile = jnp.broadcast_to(row, (16, row.shape[1])).astype(BF)
    return jnp.concatenate([tile] * (rows // 16), axis=0)


def ids(rows):
    return lax.broadcasted_iota(jnp.int32, (rows, 128), 0).astype(F32).astype(BF)


def halves(value):
    high = value.astype(BF).astype(F32)
    return high, value - high


def onehot(mask):
    return jnp.where(mask, jnp.ones((), BF), jnp.zeros((), BF))


def place(device):
    return (device // GRIDS, device % GRIDS)


def wait_for(view, semaphore):
    pltpu.make_async_copy(view, view, semaphore).wait()


def send_all(me, source, target, rows, send_sem, recv_sem):
    def one(step, carry):
        q = lax.rem(me + step, DEVICES)
        pltpu.make_async_remote_copy(
            src_ref=source.at[q, pl.ds(0, rows)],
            dst_ref=target.at[me, pl.ds(0, rows)],
            send_sem=send_sem,
            recv_sem=recv_sem,
            device_id=place(q),
            device_id_type=MESH,
        ).start()
        return carry

    lax.fori_loop(1, DEVICES, one, 0)
    pltpu.make_async_copy(source.at[me, pl.ds(0, rows)], target.at[me, pl.ds(0, rows)], recv_sem).start()


def kernel(
    adj, cell, nid, donor, weight, count, diag_hbm, face_hbm, met_hbm,
    product, sens,
    diag, face, met, table, counts, acc,
    pay, recv, part01, got01, part2, got2, halo_out, halo_in,
    local_sem, send_sem, recv_sem, halo_send, halo_recv,
):
    dom, grid = lax.axis_index("dom"), lax.axis_index("grid")
    me = dom * GRIDS + grid
    load_face = pltpu.make_async_copy(face_hbm, face, local_sem.at[0])
    load_met = pltpu.make_async_copy(met_hbm, met, local_sem.at[1])
    load_diag = pltpu.make_async_copy(diag_hbm, diag, local_sem.at[2])
    load_face.start()
    load_met.start()
    load_diag.start()
    barrier = pltpu.get_barrier_semaphore()

    def greet(step, carry):
        q = lax.rem(me + step, DEVICES)
        pl.semaphore_signal(barrier, inc=1, device_id=place(q), device_id_type=MESH)
        return carry

    lax.fori_loop(1, DEVICES, greet, 0)

    for v in range(6):
        high, low = halves(adj[v])
        table[v * 128:(v + 1) * 128, :128] = high.astype(BF)
        table[v * 128:(v + 1) * 128, 128:] = low.astype(BF)
    counts[...] = jnp.broadcast_to(count[...].astype(F32), (128, 128)).T
    ids64, ids128, ids256 = ids(64), ids(128), ids(256)
    row_ids = lax.broadcasted_iota(jnp.int32, (128, 128), 0)
    lane_ids = lax.broadcasted_iota(jnp.int32, (128, 128), 1)

    def fringe(block, carry):
        cells = cell[pl.ds(block * 8, 8), :]
        rows, lanes = cells >> 7, (cells & 127).astype(F32)
        for pair in range(4):
            js = (2 * pair, 2 * pair + 1)
            pick = jnp.concatenate([onehot(ids128 == spread(lanes[j:j + 1], 128)) for j in js], 1)
            pick = jnp.concatenate([pick, pick], 0)
            hits = [row_ids == jnp.broadcast_to(rows[j:j + 1], (128, 128)) for j in js]
            for v in range(6):
                found = jnp.dot(table[v * 128:(v + 1) * 128, :], pick, preferred_element_type=F32)
                for side, j in enumerate(js):
                    mine = jnp.where(hits[side], found[:, side * 128:(side + 1) * 128], 0.0)
                    pay[block * 8 + j, v:v + 1, :] = jnp.sum(mine, axis=0, keepdims=True)
        return carry

    lax.fori_loop(0, 16, fringe, 0)

    load_face.wait()
    for side, row in ((0, 0), (1, 127)):
        edge = face[0, side, :, row, :] * adj[0, row:row + 1, :]
        for i in range(1, 6):
            edge = edge + face[i, side, :, row, :] * adj[i, row:row + 1, :]
        halo_out[side, 0:6, :] = edge

    pl.semaphore_wait(barrier, DEVICES - 1)
    send_all(me, pay, recv, 8, send_sem.at[0], recv_sem.at[0])
    halos = []
    for side, to in ((0, lax.rem(dom + DOMS - 1, DOMS)), (1, lax.rem(dom + 1, DOMS))):
        copy = pltpu.make_async_remote_copy(
            src_ref=halo_out.at[side],
            dst_ref=halo_in.at[side],
            send_sem=halo_send.at[side],
            recv_sem=halo_recv.at[side],
            device_id=(to, grid),
            device_id_type=MESH,
        )
        copy.start()
        halos.append(copy)

    load_met.wait()
    depth = 4
    zero256 = jnp.zeros((256, 128), BF)
    zero64 = jnp.zeros((64, 128), BF)

    def node_pass(xs):
        for t in range(2 * len(xs)):
            acc[t] = jnp.zeros((256, 256), F32)

        def tile(step, carry):
            k, rows8 = step // 16, pl.ds((step % 16) * 8, 8)
            n = nid[k, rows8, :]
            high = (((n >> 8) & 1) * 128 + (n >> 9)).astype(F32)
            low = (n & 255).astype(F32)
            terms = []
            for x in xs:
                term = met[0, x, k, rows8, :] * adj[0, rows8, :]
                for i in range(1, 6):
                    term = term + met[i, x, k, rows8, :] * adj[i, rows8, :]
                terms += halves(term)
            for group in range(8 // depth):
                js = range(group * depth, (group + 1) * depth)
                lows = jnp.concatenate([onehot(ids256 == spread(low[j:j + 1], 256)) for j in js], 1)
                masks = [ids256 == spread(high[j:j + 1], 256) for j in js]
                for t in range(2 * len(xs)):
                    highs = jnp.concatenate(
                        [jnp.where(m, spread(terms[t][j:j + 1], 256), zero256) for m, j in zip(masks, js)], 1
                    )
                    acc[t] += lax.dot_general(
                        highs, lows, (((1,), (1,)), ((), ())), preferred_element_type=F32
                    )
            return carry

        lax.fori_loop(0, 64, tile, 0)

    def node_store(where, slots):
        for slot in range(slots):
            for e in range(2):
                rows = slice(e * 128, (e + 1) * 128)
                both = acc[2 * slot, rows, :] + acc[2 * slot + 1, rows, :]
                for b in range(2):
                    where[:, slot * 4 + e * 2 + b, :] = both[:, b * 128:(b + 1) * 128]

    node_pass((0, 1))
    node_store(part01, 2)
    send_all(me, part01, got01, 8, send_sem.at[1], recv_sem.at[1])
    node_pass((2,))
    node_store(part2, 1)
    send_all(me, part2, got2, 4, send_sem.at[2], recv_sem.at[2])

    wait_for(recv, recv_sem.at[0])
    for t in range(3):
        acc[t] = jnp.zeros((256, 256), F32)

    def senders(block, carry):
        rows8 = pl.ds(block * 8, 8)
        cells = donor[rows8, :]
        rows, cols = cells >> 7, cells & 127
        high = (rows & 63).astype(F32)
        low = ((rows >> 6) * 128 + cols).astype(F32)
        live = lane_ids[0:8].astype(F32) < counts[rows8, :]
        weights = jnp.where(live, weight[rows8, :], 0.0)
        values = [halves(-(recv[rows8, i, :] * weights)) for i in range(6)]
        for group in range(8 // depth):
            js = range(group * depth, (group + 1) * depth)
            lows = jnp.concatenate([onehot(ids256 == spread(low[j:j + 1], 256)) for j in js], 1)
            masks = [ids64 == spread(high[j:j + 1], 64) for j in js]
            for third in range(3):
                highs = jnp.concatenate(
                    [
                        jnp.concatenate(
                            [jnp.where(m, spread(values[i][half][j:j + 1], 64), zero64) for m, j in zip(masks, js)],
                            1,
                        )
                        for i in (2 * third, 2 * third + 1)
                        for half in range(2)
                    ],
                    0,
                )
                acc[third] += lax.dot_general(
                    highs, lows, (((1,), (1,)), ((), ())), preferred_element_type=F32
                )
        return carry

    lax.fori_loop(0, 16, senders, 0)
    for i in range(6):
        start = (i % 2) * 128
        both = acc[i // 2, start:start + 64, :] + acc[i // 2, start + 64:start + 128, :]
        product[i, :64, :] = both[:, :128]
        product[i, 64:, :] = both[:, 128:]

    load_diag.wait()
    for copy in halos:
        copy.wait()
    first, last = row_ids == 0, row_ids == 127
    left, right = lane_ids == 0, lane_ids == 127

    def variable(j, carry):
        def against(block):
            total = block(0) * adj[0]
            for i in range(1, 6):
                total = total + block(i) * adj[i]
            return total

        below = jnp.where(dom == DOMS - 1, 0.0, halo_in[0, pl.ds(j, 1), :])
        above = jnp.where(dom == 0, 0.0, halo_in[1, pl.ds(j, 1), :])
        total = product[j] + against(lambda i: diag[i, j])
        up = pltpu.roll(against(lambda i: face[i, 0, j]), 127, 0)
        total = total + jnp.where(last, jnp.broadcast_to(below, (128, 128)), up)
        down = pltpu.roll(against(lambda i: face[i, 1, j]), 1, 0)
        total = total + jnp.where(first, jnp.broadcast_to(above, (128, 128)), down)
        total = total + jnp.where(right, 0.0, pltpu.roll(against(lambda i: face[i, 2, j]), 127, 1))
        total = total + jnp.where(left, 0.0, pltpu.roll(against(lambda i: face[i, 3, j]), 1, 1))
        product[j] = total
        return carry

    lax.fori_loop(0, 6, variable, 0)

    wait_for(got01, recv_sem.at[1])
    owned = jnp.sum(got01[...], axis=0)
    for x in range(2):
        for b in range(4):
            sens[x:x + 1, b * 128:(b + 1) * 128] = owned[x * 4 + b:x * 4 + b + 1, :]
    wait_for(got2.at[:, pl.ds(0, 4)], recv_sem.at[2])
    owned = jnp.sum(got2[:, 0:4, :], axis=0)
    for b in range(4):
        sens[2:3, b * 128:(b + 1) * 128] = owned[b:b + 1, :]

    others = DEVICES - 1
    wait_for(pay.at[pl.ds(0, others)], send_sem.at[0])
    wait_for(part01.at[pl.ds(0, others)], send_sem.at[1])
    wait_for(part2.at[pl.ds(0, others), pl.ds(0, 4)], send_sem.at[2])


def local(
    adjoint, jac_diag, jac_face, metric, node_id, fringe_cell, donor_cell, fringe_weight, donor_count
):
    vmem = pl.BlockSpec(memory_space=pltpu.VMEM)
    hbm = pl.BlockSpec(memory_space=pl.ANY)
    blocks = pltpu.VMEM((DEVICES, 8, 128), F32)
    product, sens = pl.pallas_call(
        kernel,
        in_specs=[vmem] * 6 + [hbm] * 3,
        out_specs=[vmem, vmem],
        out_shape=[
            jax.ShapeDtypeStruct((6, 128, 128), F32),
            jax.ShapeDtypeStruct((3, 512), F32),
        ],
        scratch_shapes=[
            pltpu.VMEM((6, 6, 128, 128), F32),
            pltpu.VMEM((6, 4, 6, 128, 128), F32),
            pltpu.VMEM((6, 3, 4, 128, 128), F32),
            pltpu.VMEM((768, 256), BF),
            pltpu.VMEM((128, 128), F32),
            pltpu.VMEM((4, 256, 256), F32),
            blocks, blocks, blocks, blocks, blocks, blocks,
            pltpu.VMEM((2, 8, 128), F32),
            pltpu.VMEM((2, 8, 128), F32),
            pltpu.SemaphoreType.DMA((3,)),
            pltpu.SemaphoreType.DMA((3,)),
            pltpu.SemaphoreType.DMA((3,)),
            pltpu.SemaphoreType.DMA((2,)),
            pltpu.SemaphoreType.DMA((2,)),
        ],
        compiler_params=pltpu.CompilerParams(
            collective_id=0, has_side_effects=True, vmem_limit_bytes=58 * 2**20
        ),
        name="adjoint_step",
    )(
        adjoint[0], fringe_cell[0], node_id[0], donor_cell[0], fringe_weight[0], donor_count,
        jac_diag[0], jac_face[0], metric[0],
    )
    return (product[None], sens)


def solution(mesh):
    in_specs = (
        P("grid", None, "dom", None),
        P("grid", None, None, "dom", None),
        P("grid", None, None, None, "dom", None),
        P("grid", None, None, None, "dom", None),
        P("grid", None, "dom", None),
        P(("dom", "grid"), None, None),
        P(("dom", "grid"), None, None),
        P(("dom", "grid"), None, None),
        P(("dom", "grid"), None),
    )
    out_specs = (P("grid", None, "dom", None), P(None, ("dom", "grid")))
    return jax.shard_map(local, mesh=mesh, in_specs=in_specs, out_specs=out_specs, check_vma=False)
```

time: 1190 us -> 116 us (0.10)
  waiting for transfers between devices: 586 us -> 0 us
  other arithmetic: 463 us -> 0 us
  Pallas kernels: 0 us -> 113 us
  local copies, waits for them, and re-layouts: 99.9 us -> 3.06 us
  starting transfers between devices: 19.5 us -> 0 us
  between operations: 14.3 us -> 0.64 us
    reduce_scatter x1 -> x0, waiting for transfers between devices: 586 us -> none  [local(): lax.psum_scatter(partial_value, ('dom', 'grid'), scatter_dimension=1, til...]
    scatter-add x2 -> x0, other arithmetic: 452 us -> none  [the longest x1 361 us: local(): partial_value = jnp.zeros((corner_terms.shape[0], node_total), jnp.float3...]
    pallas_call x0 -> x1, Pallas kernels: none -> 113 us  [local(): pl.pallas_call(kernel, in_specs=[vmem] * 6 + [hbm] * 3, out_specs=[vmem,...]
    gather x2 -> x0, local copies, waits for them, and re-layouts: 63.4 us -> none  [local(): payload = jnp.take(flat_values, fringe_cell[0], axis=1)]
    add x1 -> x0, local copies, waits for them, and re-layouts: 16.5 us -> none  [contract(): running = running + blocks[variable] * adjoint_local[variable]]
    all_to_all x1 -> x0, starting transfers between devices: 13.2 us -> none  [local(): lax.all_to_all(payload, ('dom', 'grid'), split_axis=1, concat_axis=1, til...]
  transfers between devices with their start and end apart: 4 -> 0, of which waited for: 1 -> 0; matrix products, arithmetic and copies ran while one was open for 47% -> 0% of each run, Pallas kernels for 0% -> 0%
where the time goes in v3:
time: 116 us
  Pallas kernels  113 us (97%)
  local copies, waits for them, and re-layouts  3.06 us (3%)
    pallas_call x1, Pallas kernels, local(): pl.pallas_call(kernel, in_specs=[vmem] * 6 + [hbm] * 3, out_specs=[vmem,...  113 us
    unnamed x2, local copies, waits for them, and re-layouts  3.06 us

profile of v3, /device:TPU:1, one launch (start us, length us, event | category | flops | bytes accessed | tf_op | source)
XLA Modules:
  0.0 116.3 jit_solution(1443406891614125928)
XLA Ops:
  0.6 112.6 %adjoint_step.1 = (f32[6,128,128]{2,1,0:T(8,128)}, f32[3,512]{1,0:T(4,128)}) custom-call(f32[6,128,128]{2,1,0:T(8,128)} %bitcast.13, s32[128,128]{1,0:T(8,128)} %bitcast.15, s32[4,128,128]{2,1,0:T(8,128)} %bitcast.14, s32[128,128]{1,0:T(8,128)} %bitcast.16, f32[128,128]{1,0:T(8,128)} %bitcast.17, s32[1,128]{1,0:T(1,128)} %count.1, ...), custom_call_target="tpu_custom_call" | custom-call | tf_op jit(solution)/shard_map/adjoint_step/pallas_call | solution.py:271
  113.2 1.8 %copy.13 = f32[1,6,128,128]{3,2,1,0:T(8,128)} copy(f32[1,6,128,128]{3,2,1,0:T(8,128)} %bitcast.12) | data formatting | bytes 786432
  115.0 1.3 %copy.14 = f32[3,512]{1,0:T(4,128)} copy(f32[3,512]{1,0:T(4,128)} %get-tuple-element.9) | data formatting | bytes 12288

commit v4 on v3

--- a/solution.py
+++ b/solution.py
@@ -6,6 +6,7 @@
 from jax.sharding import PartitionSpec as P
 
 BF = jnp.bfloat16
+F8 = jnp.float8_e4m3fn
 F32 = jnp.float32
 DEVICES = 128
 GRIDS = 8
@@ -18,6 +19,18 @@
     return jnp.concatenate([tile] * (rows // 16), axis=0)
 
 
+def spread8(row, kind):
+    tile = jnp.broadcast_to(row, (32, row.shape[1])).astype(kind)
+    return jnp.concatenate([tile] * 8, axis=0)
+
+
+def digits(value):
+    first = value.astype(F8).astype(F32)
+    rest = (value - first) * 16.0
+    second = rest.astype(F8).astype(F32)
+    return first, second, (rest - second) * 16.0
+
+
 def ids(rows):
     return lax.broadcasted_iota(jnp.int32, (rows, 128), 0).astype(F32).astype(BF)
 
@@ -31,29 +44,45 @@
     return jnp.where(mask, jnp.ones((), BF), jnp.zeros((), BF))
 
 
-def place(device):
-    return (device // GRIDS, device % GRIDS)
+def partner(me, step):
+    device = me + jnp.where(step == DEVICES, DEVICES // 2, step)
+    device = jnp.where(device >= DEVICES, device - DEVICES, device)
+    return device, (lax.div(device, GRIDS), lax.rem(device, GRIDS))
 
 
 def wait_for(view, semaphore):
     pltpu.make_async_copy(view, view, semaphore).wait()
 
 
-def send_all(me, source, target, rows, send_sem, recv_sem):
-    def one(step, carry):
-        q = lax.rem(me + step, DEVICES)
+class Exchange:
+    def __init__(self, me, source, target, rows, send_sem, recv_sem):
+        self.me, self.source, self.target, self.rows = me, source, target, rows
+        self.send_sem, self.recv_sem = send_sem, recv_sem
+
+    def block(self, ref, index):
+        return ref.at[index] if self.rows == 8 else ref.at[index, pl.ds(0, self.rows)]
+
+    def keep(self):
+        pltpu.make_async_copy(
+            self.block(self.source, self.me), self.block(self.target, self.me), self.recv_sem
+        ).start()
+
+    def send(self, step):
+        device, coordinates = partner(self.me, step)
         pltpu.make_async_remote_copy(
-            src_ref=source.at[q, pl.ds(0, rows)],
-            dst_ref=target.at[me, pl.ds(0, rows)],
-            send_sem=send_sem,
-            recv_sem=recv_sem,
-            device_id=place(q),
+            src_ref=self.block(self.source, device),
+            dst_ref=self.block(self.target, jnp.where(step == DEVICES, DEVICES, self.me)),
+            send_sem=self.send_sem,
+            recv_sem=self.recv_sem,
+            device_id=coordinates,
             device_id_type=MESH,
         ).start()
-        return carry
-
-    lax.fori_loop(1, DEVICES, one, 0)
-    pltpu.make_async_copy(source.at[me, pl.ds(0, rows)], target.at[me, pl.ds(0, rows)], recv_sem).start()
+
+    def wait_recv(self):
+        wait_for(self.block(self.target, pl.ds(0, DEVICES + 1)), self.recv_sem)
+
+    def wait_send(self):
+        wait_for(self.block(self.source, pl.ds(0, DEVICES)), self.send_sem)
 
 
 def kernel(
@@ -73,13 +102,6 @@
     load_diag.start()
     barrier = pltpu.get_barrier_semaphore()
 
-    def greet(step, carry):
-        q = lax.rem(me + step, DEVICES)
-        pl.semaphore_signal(barrier, inc=1, device_id=place(q), device_id_type=MESH)
-        return carry
-
-    lax.fori_loop(1, DEVICES, greet, 0)
-
     for v in range(6):
         high, low = halves(adj[v])
         table[v * 128:(v + 1) * 128, :128] = high.astype(BF)
@@ -92,15 +114,20 @@
     def fringe(block, carry):
         cells = cell[pl.ds(block * 8, 8), :]
         rows, lanes = cells >> 7, (cells & 127).astype(F32)
+        for k in range(8):
+            pl.semaphore_signal(
+                barrier, inc=1, device_id=partner(me, block * 8 + k + 1)[1], device_id_type=MESH
+            )
         for pair in range(4):
             js = (2 * pair, 2 * pair + 1)
             pick = jnp.concatenate([onehot(ids128 == spread(lanes[j:j + 1], 128)) for j in js], 1)
             pick = jnp.concatenate([pick, pick], 0)
             hits = [row_ids == jnp.broadcast_to(rows[j:j + 1], (128, 128)) for j in js]
+            found = jnp.dot(table[...], pick, preferred_element_type=F32)
             for v in range(6):
-                found = jnp.dot(table[v * 128:(v + 1) * 128, :], pick, preferred_element_type=F32)
                 for side, j in enumerate(js):
-                    mine = jnp.where(hits[side], found[:, side * 128:(side + 1) * 128], 0.0)
+                    mine = found[v * 128:(v + 1) * 128, side * 128:(side + 1) * 128]
+                    mine = jnp.where(hits[side], mine, 0.0)
                     pay[block * 8 + j, v:v + 1, :] = jnp.sum(mine, axis=0, keepdims=True)
         return carry
 
@@ -113,8 +140,11 @@
             edge = edge + face[i, side, :, row, :] * adj[i, row:row + 1, :]
         halo_out[side, 0:6, :] = edge
 
-    pl.semaphore_wait(barrier, DEVICES - 1)
-    send_all(me, pay, recv, 8, send_sem.at[0], recv_sem.at[0])
+    pl.semaphore_wait(barrier, DEVICES)
+    fringes = Exchange(me, pay, recv, 8, send_sem.at[0], recv_sem.at[0])
+    nodes01 = Exchange(me, part01, got01, 8, send_sem.at[1], recv_sem.at[1])
+    nodes2 = Exchange(me, part2, got2, 4, send_sem.at[2], recv_sem.at[2])
+    fringes.keep()
     halos = []
     for side, to in ((0, lax.rem(dom + DOMS - 1, DOMS)), (1, lax.rem(dom + 1, DOMS))):
         copy = pltpu.make_async_remote_copy(
@@ -129,32 +159,54 @@
         halos.append(copy)
 
     load_met.wait()
+
+    def corners(block, peaks):
+        rows8 = pl.ds(block * 8, 8)
+        values = [adj[i, rows8, :] for i in range(6)]
+        found = []
+        for x in range(3):
+            peak = peaks[x]
+            for k in range(4):
+                term = met[0, x, k, rows8, :] * values[0]
+                for i in range(1, 6):
+                    term = term + met[i, x, k, rows8, :] * values[i]
+                met[0, x, k, rows8, :] = term
+                peak = jnp.maximum(peak, jnp.abs(term))
+            found.append(peak)
+        return tuple(found)
+
+    peaks = lax.fori_loop(0, 16, corners, (jnp.zeros((8, 128), F32),) * 3)
+    peaks = [jnp.maximum(jnp.max(peak, keepdims=True), 1e-30) for peak in peaks]
+
     depth = 4
-    zero256 = jnp.zeros((256, 128), BF)
     zero64 = jnp.zeros((64, 128), BF)
-
-    def node_pass(xs):
-        for t in range(2 * len(xs)):
+    ids8 = (lax.broadcasted_iota(jnp.int32, (256, 128), 0) - 128).astype(jnp.int8)
+    one8, zero8 = jnp.ones((), F8), jnp.zeros((), F8)
+
+    def node_pass(xs, exchange):
+        for t in range(3 * len(xs)):
             acc[t] = jnp.zeros((256, 256), F32)
+        scales = [jnp.broadcast_to(440.0 / peaks[x], (8, 128)) for x in xs]
 
         def tile(step, carry):
-            k, rows8 = step // 16, pl.ds((step % 16) * 8, 8)
+            exchange.send(2 * step + 1)
+            exchange.send(2 * step + 2)
+            k, rows8 = lax.div(step, 16), pl.ds(lax.rem(step, 16) * 8, 8)
             n = nid[k, rows8, :]
-            high = (((n >> 8) & 1) * 128 + (n >> 9)).astype(F32)
-            low = (n & 255).astype(F32)
+            high = ((n >> 8) & 1) * 128 + (n >> 9) - 128
+            low = (n & 255) - 128
             terms = []
-            for x in xs:
-                term = met[0, x, k, rows8, :] * adj[0, rows8, :]
-                for i in range(1, 6):
-                    term = term + met[i, x, k, rows8, :] * adj[i, rows8, :]
-                terms += halves(term)
+            for x, scale in zip(xs, scales):
+                terms += digits(met[0, x, k, rows8, :] * scale)
             for group in range(8 // depth):
                 js = range(group * depth, (group + 1) * depth)
-                lows = jnp.concatenate([onehot(ids256 == spread(low[j:j + 1], 256)) for j in js], 1)
-                masks = [ids256 == spread(high[j:j + 1], 256) for j in js]
-                for t in range(2 * len(xs)):
+                lows = jnp.concatenate(
+                    [jnp.where(ids8 == spread8(low[j:j + 1], jnp.int8), one8, zero8) for j in js], 1
+                )
+                masks = [ids8 == spread8(high[j:j + 1], jnp.int8) for j in js]
+                for t in range(3 * len(xs)):
                     highs = jnp.concatenate(
-                        [jnp.where(m, spread(terms[t][j:j + 1], 256), zero256) for m, j in zip(masks, js)], 1
+                        [jnp.where(m, spread8(terms[t][j:j + 1], F8), zero8) for m, j in zip(masks, js)], 1
                     )
                     acc[t] += lax.dot_general(
                         highs, lows, (((1,), (1,)), ((), ())), preferred_element_type=F32
@@ -163,26 +215,30 @@
 
         lax.fori_loop(0, 64, tile, 0)
 
-    def node_store(where, slots):
-        for slot in range(slots):
+    def node_store(where, xs):
+        for slot, x in enumerate(xs):
+            unit = peaks[x] * (1.0 / 440.0)
             for e in range(2):
                 rows = slice(e * 128, (e + 1) * 128)
-                both = acc[2 * slot, rows, :] + acc[2 * slot + 1, rows, :]
+                total = acc[3 * slot + 1, rows, :] + acc[3 * slot + 2, rows, :] * (1.0 / 16.0)
+                total = (acc[3 * slot, rows, :] + total * (1.0 / 16.0)) * unit
                 for b in range(2):
-                    where[:, slot * 4 + e * 2 + b, :] = both[:, b * 128:(b + 1) * 128]
-
-    node_pass((0, 1))
-    node_store(part01, 2)
-    send_all(me, part01, got01, 8, send_sem.at[1], recv_sem.at[1])
-    node_pass((2,))
-    node_store(part2, 1)
-    send_all(me, part2, got2, 4, send_sem.at[2], recv_sem.at[2])
-
-    wait_for(recv, recv_sem.at[0])
+                    where[0:128, slot * 4 + e * 2 + b, :] = total[:, b * 128:(b + 1) * 128]
+
+    node_pass((0, 1), fringes)
+    node_store(part01, (0, 1))
+    nodes01.keep()
+    node_pass((2,), nodes01)
+    node_store(part2, (2,))
+    nodes2.keep()
+
+    fringes.wait_recv()
     for t in range(3):
         acc[t] = jnp.zeros((256, 256), F32)
 
     def senders(block, carry):
+        for k in range(8):
+            nodes2.send(block * 8 + k + 1)
         rows8 = pl.ds(block * 8, 8)
         cells = donor[rows8, :]
         rows, cols = cells >> 7, cells & 127
@@ -246,20 +302,18 @@
 
     lax.fori_loop(0, 6, variable, 0)
 
-    wait_for(got01, recv_sem.at[1])
-    owned = jnp.sum(got01[...], axis=0)
+    nodes01.wait_recv()
+    owned = jnp.sum(got01[0:128], axis=0)
     for x in range(2):
         for b in range(4):
             sens[x:x + 1, b * 128:(b + 1) * 128] = owned[x * 4 + b:x * 4 + b + 1, :]
-    wait_for(got2.at[:, pl.ds(0, 4)], recv_sem.at[2])
-    owned = jnp.sum(got2[:, 0:4, :], axis=0)
+    nodes2.wait_recv()
+    owned = jnp.sum(got2[0:128, 0:4, :], axis=0)
     for b in range(4):
         sens[2:3, b * 128:(b + 1) * 128] = owned[b:b + 1, :]
 
-    others = DEVICES - 1
-    wait_for(pay.at[pl.ds(0, others)], send_sem.at[0])
-    wait_for(part01.at[pl.ds(0, others)], send_sem.at[1])
-    wait_for(part2.at[pl.ds(0, others), pl.ds(0, 4)], send_sem.at[2])
+    for exchange in (fringes, nodes01, nodes2):
+        exchange.wait_send()
 
 
 def local(
@@ -267,7 +321,8 @@
 ):
     vmem = pl.BlockSpec(memory_space=pltpu.VMEM)
     hbm = pl.BlockSpec(memory_space=pl.ANY)
-    blocks = pltpu.VMEM((DEVICES, 8, 128), F32)
+    source = pltpu.VMEM((DEVICES, 8, 128), F32)
+    target = pltpu.VMEM((DEVICES + 1, 8, 128), F32)
     product, sens = pl.pallas_call(
         kernel,
         in_specs=[vmem] * 6 + [hbm] * 3,
@@ -282,8 +337,8 @@
             pltpu.VMEM((6, 3, 4, 128, 128), F32),
             pltpu.VMEM((768, 256), BF),
             pltpu.VMEM((128, 128), F32),
-            pltpu.VMEM((4, 256, 256), F32),
-            blocks, blocks, blocks, blocks, blocks, blocks,
+            pltpu.VMEM((6, 256, 256), F32),
+            source, target, source, target, source, target,
             pltpu.VMEM((2, 8, 128), F32),
             pltpu.VMEM((2, 8, 128), F32),
             pltpu.SemaphoreType.DMA((3,)),

time: 116 us -> 100 us (0.86)
  Pallas kernels: 113 us -> 96.1 us
    pallas_call x1, Pallas kernels: 113 us -> 96.1 us  [local(): pl.pallas_call(kernel, in_specs=[vmem] * 6 + [hbm] * 3, out_specs=[vmem,...]
where the time goes in v4:
time: 100 us; the launch traced here: 99.8 us
  Pallas kernels  96.1 us (96%)
  local copies, waits for them, and re-layouts  3.06 us (3%)
    pallas_call x1, Pallas kernels, local(): pl.pallas_call(kernel, in_specs=[vmem] * 6 + [hbm] * 3, out_specs=[vmem,...  96.1 us
    unnamed x2, local copies, waits for them, and re-layouts  3.06 us

profile of v4, /device:TPU:1, one launch (start us, length us, event | category | flops | bytes accessed | tf_op | source)
XLA Modules:
  0.0 99.8 jit_solution(17123627642273512465)
XLA Ops:
  0.6 96.1 %adjoint_step.1 = (f32[6,128,128]{2,1,0:T(8,128)}, f32[3,512]{1,0:T(4,128)}) custom-call(f32[6,128,128]{2,1,0:T(8,128)} %bitcast.13, s32[128,128]{1,0:T(8,128)} %bitcast.15, s32[4,128,128]{2,1,0:T(8,128)} %bitcast.14, s32[128,128]{1,0:T(8,128)} %bitcast.16, f32[128,128]{1,0:T(8,128)} %bitcast.17, s32[1,128]{1,0:T(1,128)} %count.1, ...), custom_call_target="tpu_custom_call" | custom-call | tf_op jit(solution)/shard_map/adjoint_step/pallas_call | solution.py:326
  96.7 1.8 %copy.13 = f32[1,6,128,128]{3,2,1,0:T(8,128)} copy(f32[1,6,128,128]{3,2,1,0:T(8,128)} %bitcast.12) | data formatting | bytes 786432
  98.5 1.3 %copy.14 = f32[3,512]{1,0:T(4,128)} copy(f32[3,512]{1,0:T(4,128)} %get-tuple-element.9) | data formatting | bytes 12288

commit v5 on v4

--- a/solution.py
+++ b/solution.py
@@ -8,6 +8,11 @@
 BF = jnp.bfloat16
 F8 = jnp.float8_e4m3fn
 F32 = jnp.float32
+NODE_DEPTH = 8
+DONOR_DEPTH = 8
+FRINGE_STEP = 2
+DONOR_STEP = 4
+NODE_STEP = 2
 DEVICES = 128
 GRIDS = 8
 DOMS = 16
@@ -110,28 +115,39 @@
     ids64, ids128, ids256 = ids(64), ids(128), ids(256)
     row_ids = lax.broadcasted_iota(jnp.int32, (128, 128), 0)
     lane_ids = lax.broadcasted_iota(jnp.int32, (128, 128), 1)
-
-    def fringe(block, carry):
+    sublanes = lax.broadcasted_iota(jnp.int32, (8, 128), 0)
+
+    def fringe(step, carry):
+        for k in range(8 * FRINGE_STEP):
+            pl.semaphore_signal(
+                barrier, inc=1, device_id=partner(me, step * 8 * FRINGE_STEP + k + 1)[1], device_id_type=MESH
+            )
+        for u in range(FRINGE_STEP):
+            fringe_rows(step * FRINGE_STEP + u)
+        return carry
+
+    def fringe_rows(block):
         cells = cell[pl.ds(block * 8, 8), :]
         rows, lanes = cells >> 7, (cells & 127).astype(F32)
-        for k in range(8):
-            pl.semaphore_signal(
-                barrier, inc=1, device_id=partner(me, block * 8 + k + 1)[1], device_id_type=MESH
-            )
         for pair in range(4):
             js = (2 * pair, 2 * pair + 1)
             pick = jnp.concatenate([onehot(ids128 == spread(lanes[j:j + 1], 128)) for j in js], 1)
             pick = jnp.concatenate([pick, pick], 0)
-            hits = [row_ids == jnp.broadcast_to(rows[j:j + 1], (128, 128)) for j in js]
+            wide = [jnp.broadcast_to(rows[j:j + 1], (8, 128)) for j in js]
+            bands = [[(w >> 3) == band for band in range(16)] for w in wide]
+            hits = [sublanes == (w & 7) for w in wide]
             found = jnp.dot(table[...], pick, preferred_element_type=F32)
             for v in range(6):
                 for side, j in enumerate(js):
-                    mine = found[v * 128:(v + 1) * 128, side * 128:(side + 1) * 128]
+                    columns = slice(side * 128, (side + 1) * 128)
+                    mine = found[v * 128:v * 128 + 8, columns]
+                    for band in range(1, 16):
+                        start = v * 128 + band * 8
+                        mine = jnp.where(bands[side][band], found[start:start + 8, columns], mine)
                     mine = jnp.where(hits[side], mine, 0.0)
                     pay[block * 8 + j, v:v + 1, :] = jnp.sum(mine, axis=0, keepdims=True)
-        return carry
-
-    lax.fori_loop(0, 16, fringe, 0)
+
+    lax.fori_loop(0, 16 // FRINGE_STEP, fringe, 0)
 
     load_face.wait()
     for side, row in ((0, 0), (1, 127)):
@@ -178,7 +194,6 @@
     peaks = lax.fori_loop(0, 16, corners, (jnp.zeros((8, 128), F32),) * 3)
     peaks = [jnp.maximum(jnp.max(peak, keepdims=True), 1e-30) for peak in peaks]
 
-    depth = 4
     zero64 = jnp.zeros((64, 128), BF)
     ids8 = (lax.broadcasted_iota(jnp.int32, (256, 128), 0) - 128).astype(jnp.int8)
     one8, zero8 = jnp.ones((), F8), jnp.zeros((), F8)
@@ -189,17 +204,22 @@
         scales = [jnp.broadcast_to(440.0 / peaks[x], (8, 128)) for x in xs]
 
         def tile(step, carry):
-            exchange.send(2 * step + 1)
-            exchange.send(2 * step + 2)
-            k, rows8 = lax.div(step, 16), pl.ds(lax.rem(step, 16) * 8, 8)
+            for k in range(8 * NODE_STEP):
+                exchange.send(8 * NODE_STEP * step + k + 1)
+            for u in range(NODE_STEP):
+                for k in range(4):
+                    corner(k, pl.ds((step * NODE_STEP + u) * 8, 8))
+            return carry
+
+        def corner(k, rows8):
             n = nid[k, rows8, :]
             high = ((n >> 8) & 1) * 128 + (n >> 9) - 128
             low = (n & 255) - 128
             terms = []
             for x, scale in zip(xs, scales):
                 terms += digits(met[0, x, k, rows8, :] * scale)
-            for group in range(8 // depth):
-                js = range(group * depth, (group + 1) * depth)
+            for group in range(8 // NODE_DEPTH):
+                js = range(group * NODE_DEPTH, (group + 1) * NODE_DEPTH)
                 lows = jnp.concatenate(
                     [jnp.where(ids8 == spread8(low[j:j + 1], jnp.int8), one8, zero8) for j in js], 1
                 )
@@ -211,9 +231,8 @@
                     acc[t] += lax.dot_general(
                         highs, lows, (((1,), (1,)), ((), ())), preferred_element_type=F32
                     )
-            return carry
-
-        lax.fori_loop(0, 64, tile, 0)
+
+        lax.fori_loop(0, 16 // NODE_STEP, tile, 0)
 
     def node_store(where, xs):
         for slot, x in enumerate(xs):
@@ -236,9 +255,14 @@
     for t in range(3):
         acc[t] = jnp.zeros((256, 256), F32)
 
-    def senders(block, carry):
-        for k in range(8):
-            nodes2.send(block * 8 + k + 1)
+    def senders(step, carry):
+        for k in range(8 * DONOR_STEP):
+            nodes2.send(step * 8 * DONOR_STEP + k + 1)
+        for u in range(DONOR_STEP):
+            donors(step * DONOR_STEP + u)
+        return carry
+
+    def donors(block):
         rows8 = pl.ds(block * 8, 8)
         cells = donor[rows8, :]
         rows, cols = cells >> 7, cells & 127
@@ -247,8 +271,8 @@
         live = lane_ids[0:8].astype(F32) < counts[rows8, :]
         weights = jnp.where(live, weight[rows8, :], 0.0)
         values = [halves(-(recv[rows8, i, :] * weights)) for i in range(6)]
-        for group in range(8 // depth):
-            js = range(group * depth, (group + 1) * depth)
+        for group in range(8 // DONOR_DEPTH):
+            js = range(group * DONOR_DEPTH, (group + 1) * DONOR_DEPTH)
             lows = jnp.concatenate([onehot(ids256 == spread(low[j:j + 1], 256)) for j in js], 1)
             masks = [ids64 == spread(high[j:j + 1], 64) for j in js]
             for third in range(3):
@@ -266,9 +290,8 @@
                 acc[third] += lax.dot_general(
                     highs, lows, (((1,), (1,)), ((), ())), preferred_element_type=F32
                 )
-        return carry
-
-    lax.fori_loop(0, 16, senders, 0)
+
+    lax.fori_loop(0, 16 // DONOR_STEP, senders, 0)
     for i in range(6):
         start = (i % 2) * 128
         both = acc[i // 2, start:start + 64, :] + acc[i // 2, start + 64:start + 128, :]

time: 100 us -> 78.2 us (0.78)
  Pallas kernels: 96.1 us -> 74.3 us
    pallas_call x1, Pallas kernels: 96.1 us -> 74.3 us  [local(): pl.pallas_call(kernel, in_specs=[vmem] * 6 + [hbm] * 3, out_specs=[vmem,...]
where the time goes in v5:
time: 78.2 us; the launch traced here: 78 us
  Pallas kernels  74.3 us (95%)
  local copies, waits for them, and re-layouts  3.06 us (4%)
    pallas_call x1, Pallas kernels, local(): pl.pallas_call(kernel, in_specs=[vmem] * 6 + [hbm] * 3, out_specs=[vmem,...  74.3 us
    unnamed x2, local copies, waits for them, and re-layouts  3.06 us

profile of v5, /device:TPU:1, one launch (start us, length us, event | category | flops | bytes accessed | tf_op | source)
XLA Modules:
  0.0 78.0 jit_solution(15993499180660538049)
XLA Ops:
  0.6 74.3 %adjoint_step.1 = (f32[6,128,128]{2,1,0:T(8,128)}, f32[3,512]{1,0:T(4,128)}) custom-call(f32[6,128,128]{2,1,0:T(8,128)} %bitcast.13, s32[128,128]{1,0:T(8,128)} %bitcast.15, s32[4,128,128]{2,1,0:T(8,128)} %bitcast.14, s32[128,128]{1,0:T(8,128)} %bitcast.16, f32[128,128]{1,0:T(8,128)} %bitcast.17, s32[1,128]{1,0:T(1,128)} %count.1, ...), custom_call_target="tpu_custom_call" | custom-call | tf_op jit(solution)/shard_map/adjoint_step/pallas_call | solution.py:349
  75.0 1.8 %copy.13 = f32[1,6,128,128]{3,2,1,0:T(8,128)} copy(f32[1,6,128,128]{3,2,1,0:T(8,128)} %bitcast.12) | data formatting | bytes 786432
  76.7 1.3 %copy.14 = f32[3,512]{1,0:T(4,128)} copy(f32[3,512]{1,0:T(4,128)} %get-tuple-element.9) | data formatting | bytes 12288

commit v6 on v5

--- a/solution.py
+++ b/solution.py
@@ -10,9 +10,9 @@
 F32 = jnp.float32
 NODE_DEPTH = 8
 DONOR_DEPTH = 8
-FRINGE_STEP = 2
-DONOR_STEP = 4
-NODE_STEP = 2
+FRINGE_STEP = 4
+DONOR_STEP = 8
+NODE_STEP = 4
 DEVICES = 128
 GRIDS = 8
 DOMS = 16
@@ -107,6 +107,15 @@
     load_diag.start()
     barrier = pltpu.get_barrier_semaphore()
 
+    def greet(step, carry):
+        for k in range(16):
+            pl.semaphore_signal(
+                barrier, inc=1, device_id=partner(me, step * 16 + k + 1)[1], device_id_type=MESH
+            )
+        return carry
+
+    lax.fori_loop(0, 8, greet, 0)
+
     for v in range(6):
         high, low = halves(adj[v])
         table[v * 128:(v + 1) * 128, :128] = high.astype(BF)
@@ -118,10 +127,6 @@
     sublanes = lax.broadcasted_iota(jnp.int32, (8, 128), 0)
 
     def fringe(step, carry):
-        for k in range(8 * FRINGE_STEP):
-            pl.semaphore_signal(
-                barrier, inc=1, device_id=partner(me, step * 8 * FRINGE_STEP + k + 1)[1], device_id_type=MESH
-            )
         for u in range(FRINGE_STEP):
             fringe_rows(step * FRINGE_STEP + u)
         return carry
@@ -156,6 +161,26 @@
             edge = edge + face[i, side, :, row, :] * adj[i, row:row + 1, :]
         halo_out[side, 0:6, :] = edge
 
+    load_met.wait()
+
+    def corners(block, peaks):
+        rows8 = pl.ds(block * 8, 8)
+        values = [adj[i, rows8, :] for i in range(6)]
+        found = []
+        for x in range(3):
+            peak = peaks[x]
+            for k in range(4):
+                term = met[0, x, k, rows8, :] * values[0]
+                for i in range(1, 6):
+                    term = term + met[i, x, k, rows8, :] * values[i]
+                met[0, x, k, rows8, :] = term
+                peak = jnp.maximum(peak, jnp.abs(term))
+            found.append(peak)
+        return tuple(found)
+
+    peaks = lax.fori_loop(0, 16, corners, (jnp.zeros((8, 128), F32),) * 3)
+    peaks = [jnp.maximum(jnp.max(peak, keepdims=True), 1e-30) for peak in peaks]
+
     pl.semaphore_wait(barrier, DEVICES)
     fringes = Exchange(me, pay, recv, 8, send_sem.at[0], recv_sem.at[0])
     nodes01 = Exchange(me, part01, got01, 8, send_sem.at[1], recv_sem.at[1])
@@ -173,26 +198,6 @@
         )
         copy.start()
         halos.append(copy)
-
-    load_met.wait()
-
-    def corners(block, peaks):
-        rows8 = pl.ds(block * 8, 8)
-        values = [adj[i, rows8, :] for i in range(6)]
-        found = []
-        for x in range(3):
-            peak = peaks[x]
-            for k in range(4):
-                term = met[0, x, k, rows8, :] * values[0]
-                for i in range(1, 6):
-                    term = term + met[i, x, k, rows8, :] * values[i]
-                met[0, x, k, rows8, :] = term
-                peak = jnp.maximum(peak, jnp.abs(term))
-            found.append(peak)
-        return tuple(found)
-
-    peaks = lax.fori_loop(0, 16, corners, (jnp.zeros((8, 128), F32),) * 3)
-    peaks = [jnp.maximum(jnp.max(peak, keepdims=True), 1e-30) for peak in peaks]
 
     zero64 = jnp.zeros((64, 128), BF)
     ids8 = (lax.broadcasted_iota(jnp.int32, (256, 128), 0) - 128).astype(jnp.int8)

time: 78.2 us -> 73.3 us (0.937)
  Pallas kernels: 74.3 us -> 69.4 us
    pallas_call x1, Pallas kernels: 74.3 us -> 69.4 us  [local(): pl.pallas_call(kernel, in_specs=[vmem] * 6 + [hbm] * 3, out_specs=[vmem,...]
where the time goes in v6:
time: 73.3 us; the launch traced here: 73.1 us
  Pallas kernels  69.4 us (95%)
  local copies, waits for them, and re-layouts  3.06 us (4%)
    pallas_call x1, Pallas kernels, local(): pl.pallas_call(kernel, in_specs=[vmem] * 6 + [hbm] * 3, out_specs=[vmem,...  69.4 us
    unnamed x2, local copies, waits for them, and re-layouts  3.06 us

profile of v6, /device:TPU:1, one launch (start us, length us, event | category | flops | bytes accessed | tf_op | source)
XLA Modules:
  0.0 73.1 jit_solution(17068284933784711562)
XLA Ops:
  0.6 69.4 %adjoint_step.1 = (f32[6,128,128]{2,1,0:T(8,128)}, f32[3,512]{1,0:T(4,128)}) custom-call(f32[6,128,128]{2,1,0:T(8,128)} %bitcast.13, s32[128,128]{1,0:T(8,128)} %bitcast.15, s32[4,128,128]{2,1,0:T(8,128)} %bitcast.14, s32[128,128]{1,0:T(8,128)} %bitcast.16, f32[128,128]{1,0:T(8,128)} %bitcast.17, s32[1,128]{1,0:T(1,128)} %count.1, ...), custom_call_target="tpu_custom_call" | custom-call | tf_op jit(solution)/shard_map/adjoint_step/pallas_call | solution.py:354
  70.0 1.8 %copy.13 = f32[1,6,128,128]{3,2,1,0:T(8,128)} copy(f32[1,6,128,128]{3,2,1,0:T(8,128)} %bitcast.12) | data formatting | bytes 786432
  71.8 1.3 %copy.14 = f32[3,512]{1,0:T(4,128)} copy(f32[3,512]{1,0:T(4,128)} %get-tuple-element.9) | data formatting | bytes 12288
